TPU v7x, 32 devices: a whole 2x2x4 slice. The times are simulated.
32 devices in a mesh: seq: 2 (over y), row: 4 (over x, core), col: 4 (over z).
Axes of the slice: x: 2, y: 2, z: 4, core: 2. Of those that a mesh axis runs over, the one named last changes fastest.
Arguments:
- tokens: bfloat16 [4096, 5376], P(('seq', 'row'), 'col'), may hold values from -6 to 6
- w_query: bfloat16 [5376, 4096], P(('seq', 'row'), 'col'), may hold values from -0.078125 to 0.078125
- key_weight: bfloat16 [5376, 2048], P(('seq', 'row'), 'col'), may hold values from -0.078125 to 0.078125
- value_weight: bfloat16 [5376, 2048], P(('seq', 'row'), 'col'), may hold values from -0.078125 to 0.078125
- w_output: bfloat16 [4096, 5376], P(('seq', 'row'), 'col'), may hold values from -0.09375 to 0.09375
- query_gain: float32 [128], replicated, may hold values from 0.5 to 8
- key_gain: float32 [128], replicated, may hold values from 0.5 to 8
Outputs:
- attended: bfloat16 [4096, 5376], P(('seq', 'row'), 'col')
All inputs are finite; a program needn't handle non-finite values.
Results may differ from a plain program's by a relative error of at most 0.0085.
The roundings to bfloat16 on the way count: a program that leaves them out, or rounds other values in their place, can miss the bound.
Values may be sent and summed in bfloat16 or wider, within the bound.
A program may use at most 128 MiB of HBM per device.

v0:
```python
import jax
import jax.numpy as jnp
from jax import lax
from jax.sharding import PartitionSpec as P

HEAD_SIZE = 128
WINDOW_KEYS = 1024
query_scale = 168.0 ** (-0.5)


def shifted(block, axis, distance):
    devices = range(lax.axis_size(axis))
    route = [(i - distance, i) for i in devices if i - distance in devices]
    return lax.ppermute(block, axis, route)


def head_norm(block, gain):
    mean_square = jnp.mean(block * block, axis=-1, keepdims=True)
    return block * lax.rsqrt(mean_square + 1e-06) * gain


def rotate(block, positions):
    half = block.shape[-1] // 2
    freqs = 10000.0 ** (-(jnp.arange(half, dtype=jnp.float32) * 2.0 / block.shape[-1]))
    angles = positions.astype(jnp.float32)[:, None] * freqs[None, :]
    cosine = jnp.cos(angles)[:, None, :]
    sine = jnp.sin(angles)[:, None, :]
    first = block[..., :half]
    second = block[..., half:]
    return jnp.concatenate(
        [first * cosine - second * sine, second * cosine + first * sine], axis=-1
    )


def attend(queries, key_states, value_states, qpos, kpos):
    rows = queries.shape[0]
    kv_heads = key_states.shape[1]
    grouped = queries.reshape(rows, kv_heads, 2, HEAD_SIZE)
    scores = (
        jnp.einsum("bhgd,khd->hgbk", grouped, key_states, preferred_element_type=jnp.float32)
        * query_scale
    )
    gap = qpos[:, None] - kpos[None, :]
    valid = (kpos[None, :] >= 0) & (gap >= 0) & (gap < WINDOW_KEYS)
    scores = jnp.where(valid[None, None], scores, -1e30)
    top = jnp.max(scores, axis=-1, keepdims=True)
    weights = jnp.exp(scores - top)
    weights = (weights / jnp.sum(weights, axis=-1, keepdims=True)).astype(jnp.bfloat16)
    mixed = jnp.einsum("hgbk,khd->bhgd", weights, value_states, preferred_element_type=jnp.float32)
    return mixed.astype(jnp.bfloat16).reshape(rows, kv_heads * 2 * HEAD_SIZE)


def shards(tokens, w_query, key_weight, value_weight, w_output, query_gain, key_gain):
    rows = tokens.shape[0]
    whole = lax.all_gather(tokens, "col", axis=1, tiled=True)
    columns = whole
    proj_q = jnp.dot(
        columns,
        lax.all_gather(w_query, ("seq", "row"), axis=0, tiled=True),
        preferred_element_type=jnp.float32,
    )
    projected_key = jnp.dot(
        columns,
        lax.all_gather(key_weight, ("seq", "row"), axis=0, tiled=True),
        preferred_element_type=jnp.float32,
    )
    proj_v = jnp.dot(
        columns,
        lax.all_gather(value_weight, ("seq", "row"), axis=0, tiled=True),
        preferred_element_type=jnp.float32,
    )
    base = lax.axis_index(("seq", "row")) * rows
    positions = base + jnp.arange(rows, dtype=jnp.int32)
    q_heads = proj_q.shape[1] // HEAD_SIZE
    kv_heads = projected_key.shape[1] // HEAD_SIZE
    queries = rotate(
        head_norm(proj_q.reshape(rows, q_heads, HEAD_SIZE), query_gain), positions
    ).astype(jnp.bfloat16)
    key_states = rotate(
        head_norm(projected_key.reshape(rows, kv_heads, HEAD_SIZE), key_gain), positions
    ).astype(jnp.bfloat16)
    key_flat = key_states.reshape(rows, kv_heads * HEAD_SIZE)
    value_flat = proj_v.astype(jnp.bfloat16)
    prior_one = shifted((key_flat, value_flat), ("seq", "row"), 1)
    prior_two = shifted((key_flat, value_flat), ("seq", "row"), 2)
    key_rows = jnp.concatenate([prior_two[0], prior_one[0], key_flat], axis=0).reshape(
        3 * rows, kv_heads, HEAD_SIZE
    )
    value_rows = jnp.concatenate([prior_two[1], prior_one[1], value_flat], axis=0).reshape(
        3 * rows, kv_heads, HEAD_SIZE
    )
    kpos = base - 2 * rows + jnp.arange(3 * rows, dtype=jnp.int32)
    mixed = attend(queries, key_rows, value_rows, positions, kpos)
    all_heads = lax.all_gather(mixed, "col", axis=1, tiled=True)
    columns = all_heads
    attended = jnp.dot(
        columns,
        lax.all_gather(w_output, ("seq", "row"), axis=0, tiled=True),
        preferred_element_type=jnp.float32,
    )
    return attended.astype(jnp.bfloat16)


def solution(mesh):
    return jax.shard_map(
        shards,
        mesh=mesh,
        in_specs=(
            P(("seq", "row"), "col"),
            P(("seq", "row"), "col"),
            P(("seq", "row"), "col"),
            P(("seq", "row"), "col"),
            P(("seq", "row"), "col"),
            P(),
            P(),
        ),
        out_specs=P(("seq", "row"), "col"),
        check_vma=False,
    )
```

profile of v0, /device:TPU:0, one launch (start us, length us, event | category | flops | bytes accessed | tf_op | source)
XLA Modules:
  0.0 458.2 jit_solution(17075732382961147357)
XLA Ops:
  10.0 1.0 multiply_cosine_fusion
  11.0 103.0 %all-gather.7.cloned.1.call-done = bf16[512,5376]{0,1:T(8,128)(2,1)} async-done(((bf16[512,1344]{0,1:T(8,128)(2,1)}), bf16[512,5376]{0,1:T(8,128)(2,1)}) %all-gather.7.cloned.1.call-update) | async-done | bytes 5505040 | tf_op jit(solution)/shard_map/all_gather | solution.py:55
  114.0 42.5 %all-gather.11.cloned.1.call-done = bf16[5376,512]{1,0:T(8,128)(2,1)} async-done(((bf16[672,512]{1,0:T(8,128)(2,1)}), bf16[5376,512]{1,0:T(8,128)(2,1)}) %all-gather.11.cloned.1.call-update) | async-done | bytes 5505040 | tf_op jit(solution)/shard_map/all_gather | solution.py:64
  156.5 6.7 %multiply_reduce_fusion.1 = (f32[512,4]{0,1:T(4,128)S(1)}, f32[512,512]{0,1:T(8,128)S(1)}) fusion(bf16[512,5376]{0,1:T(8,128)(2,1)} %all-gather.7.cloned.1.call-done, bf16[5376,512]{1,0:T(8,128)(2,1)} %all-gather.11.cloned.1.call-done), kind=kOutput, calls=%fused_computation.29 | convolution fusion | flops 2819094528 | bytes 12066816 | tf_op jit(solution)/shard_map/dot_general | solution.py:62
  164.9 3.4 collective-permute-start.2
  168.3 1.9 collective-permute-start.3
  170.3 39.0 %all-gather.9.cloned.1.call-done = bf16[5376,512]{1,0:T(8,128)(2,1)} async-done(((bf16[672,512]{1,0:T(8,128)(2,1)}), bf16[5376,512]{1,0:T(8,128)(2,1)}) %all-gather.9.cloned.1.call-update) | async-done | bytes 5505040 | tf_op jit(solution)/shard_map/all_gather | solution.py:69
  209.3 7.2 %convolution_convert_fusion.1 = bf16[512,512]{1,0:T(8,128)(2,1)S(1)} fusion(bf16[512,5376]{0,1:T(8,128)(2,1)} %all-gather.7.cloned.1.call-done, bf16[5376,512]{1,0:T(8,128)(2,1)} %all-gather.9.cloned.1.call-done), kind=kOutput, calls=%fused_computation.23 | convolution fusion | flops 2818834432 | bytes 11534336 | tf_op jit(solution)/shard_map/dot_general | solution.py:67
  216.5 3.1 collective-permute-start
  219.6 2.7 collective-permute-start.1
  222.2 2.0 fusion.9
  224.2 1.0 copy.32
  225.2 1.0 copy.33
  226.2 15.8 %collective-permute-done = bf16[512,512]{1,0:T(8,128)(2,1)} collective-permute-done((bf16[512,512]{1,0:T(8,128)(2,1)S(1)}, bf16[512,512]{1,0:T(8,128)(2,1)}, u32[]{:S(2)}, u32[]{:S(2)}) %collective-permute-start) | collective-permute-done | bytes 524320 | tf_op jit(solution)/shard_map/ppermute | solution.py:14
  242.0 1.3 pad_maximum_fusion
  243.3 1.6 copy.43
  244.9 44.2 %all-gather.13.cloned.1.call-done = bf16[5376,1024]{1,0:T(8,128)(2,1)} async-done(((bf16[672,1024]{1,0:T(8,128)(2,1)}), bf16[5376,1024]{1,0:T(8,128)(2,1)}) %all-gather.13.cloned.1.call-update) | async-done | bytes 11010064 | tf_op jit(solution)/shard_map/all_gather | solution.py:59
  289.1 10.3 %convolution_bitcast_fusion = f32[64,8,8,128]{3,1,2,0:T(8,128)S(1)} fusion(bf16[512,5376]{0,1:T(8,128)(2,1)} %all-gather.7.cloned.1.call-done, bf16[5376,1024]{1,0:T(8,128)(2,1)} %all-gather.13.cloned.1.call-done), kind=kOutput, calls=%fused_computation.19 | convolution fusion | flops 5637144576 | bytes 18612224 | tf_op jit(solution)/shard_map/dot_general | solution.py:57
  303.7 11.8 %fusion.11 = f32[4,1536,512,2]{2,1,3,0:T(8,128)} fusion(bf16[512,4,128]{2,0,1:T(8,128)(2,1)S(1)} %maximum_convert_fusion, bf16[512,4,128]{2,0,1:T(8,128)(2,1)S(1)} %copy-done.1, bf16[512,4,128]{2,0,1:T(8,128)(2,1)S(1)} %copy-done, bf16[512,4,2,64]{3,0,2,1:T(8,128)(2,1)S(1)} %bitcast.51, bf16[512,4,2,64]{3,0,2,1:T(8,128)(2,1)S(1)} %bitcast.53), kind=kOutput, calls=%fused_computation.30 | convolution fusion | flops 1617428480 | bytes 27787264 | tf_op jit(solution)/shard_map/bhgd,khd->hgbk/dot_general | solution.py:40
  315.6 10.5 %fusion.23 = f32[4,2,512]{2,1,0:T(2,128)S(1)} fusion(pred[512,1536]{0,1:T(8,128)(4,1)} %fusion.9, bf16[512,4,128]{2,0,1:T(8,128)(2,1)S(1)} %maximum_convert_fusion, bf16[512,4,128]{2,0,1:T(8,128)(2,1)} %copy.33, bf16[512,4,128]{2,0,1:T(8,128)(2,1)S(1)} %copy-done, bf16[512,4,2,64]{3,0,2,1:T(8,128)(2,1)S(1)} %bitcast.52, bf16[512,4,2,64]{3,0,2,1:T(8,128)(2,1)S(1)} %bitcast.54), kind=kOutput, calls=%fused_computation.47 | convolution fusion | flops 1642595840 | bytes 3424256 | tf_op jit(solution)/shard_map/sub | solution.py:47
  326.1 15.4 %fusion.10 = bf16[4,128,2,512]{3,1,2,0:T(8,128)(2,1)} fusion(bf16[1536,4,128,1]{0,2,3,1:T(8,128)(2,1)} %bitcast.55, f32[4,2,512]{2,1,0:T(2,128)S(1)} %fusion.23, f32[4,1536,512,2]{2,1,3,0:T(8,128)} %fusion.11, pred[512,1536]{0,1:T(8,128)(4,1)} %fusion.9), kind=kOutput, calls=%fused_computation.22 | convolution fusion | flops 1642599936 | bytes 28590080 | tf_op jit(solution)/shard_map/hgbk,khd->bhgd/dot_general | solution.py:49
  341.5 17.0 %all-gather.17.cloned.1.call-done = bf16[4096,1344]{0,1:T(8,128)(2,1)} async-done(((bf16[512,1344]{0,1:T(8,128)(2,1)}), bf16[4096,1344]{0,1:T(8,128)(2,1)}) %all-gather.17.cloned.1.call-update) | async-done | bytes 11010064 | tf_op jit(solution)/shard_map/all_gather | solution.py:98
  358.5 82.2 %all-gather.15.cloned.1.call-done = bf16[512,4096]{0,1:T(8,128)(2,1)} async-done(((bf16[512,1024]{0,1:T(8,128)(2,1)}), bf16[512,4096]{0,1:T(8,128)(2,1)}) %all-gather.15.cloned.1.call-update) | async-done | bytes 4194320 | tf_op jit(solution)/shard_map/all_gather | solution.py:94
  440.7 10.7 %convolution_convert_fusion = bf16[512,1344]{0,1:T(8,128)(2,1)} fusion(bf16[4096,1344]{0,1:T(8,128)(2,1)} %all-gather.17.cloned.1.call-done, bf16[512,4096]{0,1:T(8,128)(2,1)} %all-gather.15.cloned.1.call-done), kind=kOutput, calls=%fused_computation.14 | convolution fusion | flops 5637832704 | bytes 16580608 | tf_op jit(solution)/shard_map/dot_general | solution.py:96
  (43 shorter events, 9.3 us)
Async XLA Ops:
  6.5 107.5 %all-gather.7.cloned.1.call-start = ((), (), s32[]{:S(2)}) async-start(), calls=%async_computation | async-start | bytes 6881280 | tf_op jit(solution)/shard_map/all_gather | solution.py:55
  7.3 149.3 %all-gather.11.cloned.1.call-start = ((), (), s32[]{:S(2)}) async-start(), calls=%async_computation.2 | async-start | bytes 6193152 | tf_op jit(solution)/shard_map/all_gather | solution.py:64
  8.0 201.3 %all-gather.9.cloned.1.call-start = ((), (), s32[]{:S(2)}) async-start(), calls=%async_computation.1 | async-start | bytes 6193152 | tf_op jit(solution)/shard_map/all_gather | solution.py:69
  8.7 280.4 %all-gather.13.cloned.1.call-start = ((), (), s32[]{:S(2)}) async-start(), calls=%async_computation.3 | async-start | bytes 12386304 | tf_op jit(solution)/shard_map/all_gather | solution.py:59
  9.3 349.2 %all-gather.17.cloned.1.call-start = ((), (), s32[]{:S(2)}) async-start(), calls=%async_computation.5 | async-start | bytes 12386304 | tf_op jit(solution)/shard_map/all_gather | solution.py:98
  9.9 430.8 %all-gather.15.cloned.1.call-start = ((), (), s32[]{:S(2)}) async-start(), calls=%async_computation.4 | async-start | bytes 5242880 | tf_op jit(solution)/shard_map/all_gather | solution.py:94
  11.0 152.6 %copy-start.2 = (f32[128]{0:T(128)S(1)}, f32[128]{0:T(128)}, u32[]{:S(2)}) copy-start(f32[128]{0:T(128)} %param.13) | copy-start | bytes 1540
  164.9 59.3 %collective-permute-start.2 = (bf16[512,512]{0,1:T(8,128)(2,1)S(1)}, bf16[512,512]{0,1:T(8,128)(2,1)S(1)}, u32[]{:S(2)}, u32[]{:S(2)}) collective-permute-start(bf16[512,512]{0,1:T(8,128)(2,1)S(1)} %bitcast.58), channel_id=1, source_target_pairs={{0,8},{4,12},{8,16},{12,20},{16,24},{20,28},{1,9},{5,13},{9,17},{1... | collective-permute-start | bytes 1572872 | tf_op jit(solution)/shard_map/ppermute | solution.py:14
  168.3 56.9 %collective-permute-start.3 = (bf16[512,512]{0,1:T(8,128)(2,1)S(1)}, bf16[512,512]{0,1:T(8,128)(2,1)S(1)}, u32[]{:S(2)}, u32[]{:S(2)}) collective-permute-start(bf16[512,512]{0,1:T(8,128)(2,1)S(1)} %bitcast.59), channel_id=1, source_target_pairs={{0,4},{4,8},{8,12},{12,16},{16,20},{20,24},{24,28},{1,5},{5,9},{9,... | collective-permute-start | bytes 1572872 | tf_op jit(solution)/shard_map/ppermute | solution.py:14
  216.5 25.5 %collective-permute-start = (bf16[512,512]{1,0:T(8,128)(2,1)S(1)}, bf16[512,512]{1,0:T(8,128)(2,1)}, u32[]{:S(2)}, u32[]{:S(2)}) collective-permute-start(bf16[512,512]{1,0:T(8,128)(2,1)S(1)} %convolution_convert_fusion.1), channel_id=1, source_target_pairs={{0,8},{4,12},{8,16},{12,20},{16,24},{20,28},{1,9},{5,13},{9,17},{1... | collective-permute-start | bytes 1572872 | tf_op jit(solution)/shard_map/ppermute | solution.py:14
  219.6 22.5 %collective-permute-start.1 = (bf16[512,512]{1,0:T(8,128)(2,1)S(1)}, bf16[512,512]{1,0:T(8,128)(2,1)}, u32[]{:S(2)}, u32[]{:S(2)}) collective-permute-start(bf16[512,512]{1,0:T(8,128)(2,1)S(1)} %convolution_convert_fusion.1), channel_id=1, source_target_pairs={{0,4},{4,8},{8,12},{12,16},{16,20},{20,24},{24,28},{1,5},{5,9},{9,... | collective-permute-start | bytes 1572872 | tf_op jit(solution)/shard_map/ppermute | solution.py:14
  299.4 1.4 copy-start.3
  302.5 1.1 copy-start
  302.5 1.2 copy-start.1
Sparse Core Ops, SparseCore 0:
  8.9 105.0 all-gather.6
  115.9 40.5 all-gather.10
  158.4 50.8 all-gather.8
  211.0 78.0 all-gather.12
  290.8 67.6 all-gather.16
  359.9 80.7 all-gather.14
where the time goes:
time: 458 us
  waiting for transfers between devices  347 us (76%)
  matrix products  72.6 us (16%)
  between operations  13.7 us (3%)
  starting transfers between devices  11.2 us (2%)
  other arithmetic  7.75 us (2%)
  local copies, waits for them, and re-layouts  6.03 us (1%)
    all_gather x1, waiting for transfers between devices, shards(): whole = lax.all_gather(tokens, 'col', axis=1, tiled=True)  103 us
    all_gather x1, waiting for transfers between devices, shards(): all_heads = lax.all_gather(mixed, 'col', axis=1, tiled=True)  82.2 us
    all_gather x1, waiting for transfers between devices, shards(): lax.all_gather(w_query, ('seq', 'row'), axis=0, tiled=True)  44.2 us
    all_gather x1, waiting for transfers between devices, shards(): lax.all_gather(key_weight, ('seq', 'row'), axis=0, tiled=True)  42.5 us
    all_gather x1, waiting for transfers between devices, shards(): lax.all_gather(value_weight, ('seq', 'row'), axis=0, tiled=True)  39 us
    all_gather x1, waiting for transfers between devices, shards(): lax.all_gather(w_output, ('seq', 'row'), axis=0, tiled=True)  17 us
    ppermute x4, waiting for transfers between devices, shifted(): return lax.ppermute(block, axis, route)  15.8 us
    dot_general x1, matrix products, attend(): jnp.einsum('hgbk,khd->bhgd', weights, value_states, preferred_element_typ...  15.4 us
  transfers between devices with their start and end apart: 10, of which 7 were waited for; matrix products, arithmetic and copies ran while one was open for 16% of the time, Pallas kernels for 0%

commit v1 on v0

--- a/solution.py
+++ b/solution.py
@@ -6,6 +6,23 @@
 HEAD_SIZE = 128
 WINDOW_KEYS = 1024
 query_scale = 168.0 ** (-0.5)
+
+
+def balance_edge(field_in, named_axis):
+    panels = [field_in]
+    n_axis = lax.axis_size(named_axis)
+    for k0 in [*range(1, n_axis)]:
+        panels.append(
+            lax.ppermute(
+                panels[k0 - 1],
+                axis_name=named_axis,
+                perm=[(it, (it - 1) % n_axis) for it in range(n_axis)],
+            )
+        )
+    found_now = jnp.roll(
+        jnp.concatenate(panels, axis=0), lax.axis_index(named_axis) * field_in.shape[0], axis=0
+    )
+    return found_now
 
 
 def shifted(block, axis, distance):
@@ -65,9 +82,7 @@
         preferred_element_type=jnp.float32,
     )
     proj_v = jnp.dot(
-        columns,
-        lax.all_gather(value_weight, ("seq", "row"), axis=0, tiled=True),
-        preferred_element_type=jnp.float32,
+        columns, balance_edge(value_weight, ("seq", "row")), preferred_element_type=jnp.float32
     )
     base = lax.axis_index(("seq", "row")) * rows
     positions = base + jnp.arange(rows, dtype=jnp.int32)

time: 458 us -> 414 us (0.904)
  waiting for transfers between devices: 347 us -> 261 us
  starting transfers between devices: 11.2 us -> 34.8 us
  local copies, waits for them, and re-layouts: 6.03 us -> 22.8 us
    all_gather x1, waiting for transfers between devices: 103 us -> 14.9 us  [shards(): whole = lax.all_gather(tokens, 'col', axis=1, tiled=True)]
    ppermute x0 -> x7, waiting for transfers between devices: none -> 50.2 us  [balance_edge(): lax.ppermute(panels[k0 - 1], axis_name=named_axis, perm=[(it, (it - 1) %...]
    all_gather x1 -> x0, waiting for transfers between devices: 39 us -> none  [shards(): lax.all_gather(value_weight, ('seq', 'row'), axis=0, tiled=True)]
    ppermute x0 -> x7, starting transfers between devices: none -> 22.1 us  [balance_edge(): lax.ppermute(panels[k0 - 1], axis_name=named_axis, perm=[(it, (it - 1) %...]
    unnamed x9 -> x32, local copies, waits for them, and re-layouts: 1.4 us -> 15.2 us
    all_gather x1, waiting for transfers between devices: 42.5 us -> 36.2 us  [shards(): lax.all_gather(key_weight, ('seq', 'row'), axis=0, tiled=True)]
  transfers between devices with their start and end apart: 10 -> 16, of which waited for: 7 -> 13; matrix products, arithmetic and copies ran while one was open for 16% -> 23% of each run, Pallas kernels for 0% -> 0%
where the time goes in v1:
time: 414 us
  waiting for transfers between devices  261 us (63%)
  matrix products  73.8 us (18%)
  starting transfers between devices  34.8 us (8%)
  local copies, waits for them, and re-layouts  22.8 us (6%)
  between operations  13.4 us (3%)
  other arithmetic  8.69 us (2%)
    all_gather x1, waiting for transfers between devices, shards(): all_heads = lax.all_gather(mixed, 'col', axis=1, tiled=True)  82.2 us
    ppermute x7, waiting for transfers between devices, balance_edge(): lax.ppermute(panels[k0 - 1], axis_name=named_axis, perm=[(it, (it - 1) %...  50.2 us
    all_gather x1, waiting for transfers between devices, shards(): lax.all_gather(w_query, ('seq', 'row'), axis=0, tiled=True)  42.4 us
    all_gather x1, waiting for transfers between devices, shards(): lax.all_gather(key_weight, ('seq', 'row'), axis=0, tiled=True)  36.2 us
    ppermute x7, starting transfers between devices, balance_edge(): lax.ppermute(panels[k0 - 1], axis_name=named_axis, perm=[(it, (it - 1) %...  22.1 us
    all_gather x1, waiting for transfers between devices, shards(): lax.all_gather(w_output, ('seq', 'row'), axis=0, tiled=True)  17.6 us
    dot_general x1, matrix products, attend(): jnp.einsum('hgbk,khd->bhgd', weights, value_states, preferred_element_typ...  15.4 us
    unnamed x32, local copies, waits for them, and re-layouts  15.2 us
  transfers between devices with their start and end apart: 16, of which 13 were waited for; matrix products, arithmetic and copies ran while one was open for 23% of the time, Pallas kernels for 0%

profile of v1, /device:TPU:0, one launch (start us, length us, event | category | flops | bytes accessed | tf_op | source)
XLA Modules:
  0.0 414.1 jit_solution(15199809862116908650)
XLA Ops:
  9.4 3.4 collective-permute-start
  12.7 8.8 %collective-permute-done = bf16[672,512]{1,0:T(8,128)(2,1)S(1)} collective-permute-done((bf16[672,512]{1,0:T(8,128)(2,1)}, bf16[672,512]{1,0:T(8,128)(2,1)S(1)}, u32[]{:S(2)}, u32[]{:S(2)}) %collective-permute-start) | collective-permute-done | bytes 688160 | tf_op jit(solution)/shard_map/ppermute | solution.py:16
  24.2 8.5 %collective-permute-done.1 = bf16[672,512]{1,0:T(8,128)(2,1)S(1)} collective-permute-done((bf16[672,512]{1,0:T(8,128)(2,1)S(1)}, bf16[672,512]{1,0:T(8,128)(2,1)S(1)}, u32[]{:S(2)}, u32[]{:S(2)}) %collective-permute-start.1) | collective-permute-done | bytes 688160 | tf_op jit(solution)/shard_map/ppermute | solution.py:16
  32.7 3.2 collective-permute-start.2
  35.9 8.5 %collective-permute-done.2 = bf16[672,512]{1,0:T(8,128)(2,1)S(1)} collective-permute-done((bf16[672,512]{1,0:T(8,128)(2,1)S(1)}, bf16[672,512]{1,0:T(8,128)(2,1)S(1)}, u32[]{:S(2)}, u32[]{:S(2)}) %collective-permute-start.2) | collective-permute-done | bytes 688160 | tf_op jit(solution)/shard_map/ppermute | solution.py:16
  44.3 3.2 collective-permute-start.3
  47.5 8.5 %collective-permute-done.3 = bf16[672,512]{1,0:T(8,128)(2,1)S(1)} collective-permute-done((bf16[672,512]{1,0:T(8,128)(2,1)S(1)}, bf16[672,512]{1,0:T(8,128)(2,1)S(1)}, u32[]{:S(2)}, u32[]{:S(2)}) %collective-permute-start.3) | collective-permute-done | bytes 688160 | tf_op jit(solution)/shard_map/ppermute | solution.py:16
  56.0 3.2 collective-permute-start.4
  59.2 8.4 %collective-permute-done.4 = bf16[672,512]{1,0:T(8,128)(2,1)S(1)} collective-permute-done((bf16[672,512]{1,0:T(8,128)(2,1)S(1)}, bf16[672,512]{1,0:T(8,128)(2,1)S(1)}, u32[]{:S(2)}, u32[]{:S(2)}) %collective-permute-start.4) | collective-permute-done | bytes 688160 | tf_op jit(solution)/shard_map/ppermute | solution.py:16
  74.8 4.6 %collective-permute-done.5 = bf16[672,512]{1,0:T(8,128)(2,1)S(1)} collective-permute-done((bf16[672,512]{1,0:T(8,128)(2,1)S(1)}, bf16[672,512]{1,0:T(8,128)(2,1)S(1)}, u32[]{:S(2)}, u32[]{:S(2)}) %collective-permute-start.5) | collective-permute-done | bytes 688160 | tf_op jit(solution)/shard_map/ppermute | solution.py:16
  99.1 14.9 %all-gather.6.cloned.1.call-done = bf16[512,5376]{0,1:T(8,128)(2,1)} async-done(((bf16[512,1344]{0,1:T(8,128)(2,1)}), bf16[512,5376]{0,1:T(8,128)(2,1)}) %all-gather.6.cloned.1.call-update) | async-done | bytes 5505040 | tf_op jit(solution)/shard_map/all_gather | solution.py:72
  114.0 8.1 %fusion.16 = bf16[512,512]{1,0:T(8,128)(2,1)} fusion(bf16[512,5376]{0,1:T(8,128)(2,1)} %all-gather.6.cloned.1.call-done, bf16[10752,512]{1,0:T(8,128)(2,1)} %constant_dynamic-update-slice_fusion, s32[]{:T(128)S(6)} %select_n.18), kind=kOutput, calls=%fused_computation.26 | convolution fusion | flops 2818834432 | bytes 11534340 | tf_op jit(solution)/shard_map/dot_general | solution.py:84
  122.2 4.3 %collective-permute-start.7 = (bf16[512,512]{1,0:T(8,128)(2,1)}, bf16[512,512]{1,0:T(8,128)(2,1)}, u32[]{:S(2)}, u32[]{:S(2)}) collective-permute-start(bf16[512,512]{1,0:T(8,128)(2,1)} %fusion.16), channel_id=1, source_target_pairs={{0,8},{4,12},{8,16},{12,20},{16,24},{20,28},{1,9},{5,13},{9,17},{1... | collective-permute-start | bytes 1572872 | tf_op jit(solution)/shard_map/ppermute | solution.py:31
  128.9 36.2 %all-gather.8.cloned.1.call-done = bf16[5376,512]{1,0:T(8,128)(2,1)} async-done(((bf16[672,512]{1,0:T(8,128)(2,1)}), bf16[5376,512]{1,0:T(8,128)(2,1)}) %all-gather.8.cloned.1.call-update) | async-done | bytes 5505040 | tf_op jit(solution)/shard_map/all_gather | solution.py:81
  165.1 6.7 %multiply_reduce_fusion.1 = (f32[512,4]{0,1:T(4,128)S(1)}, f32[512,512]{0,1:T(8,128)S(1)}) fusion(bf16[512,5376]{0,1:T(8,128)(2,1)} %all-gather.6.cloned.1.call-done, bf16[5376,512]{1,0:T(8,128)(2,1)} %all-gather.8.cloned.1.call-done), kind=kOutput, calls=%fused_computation.32 | convolution fusion | flops 2819094528 | bytes 12066816 | tf_op jit(solution)/shard_map/dot_general | solution.py:79
  184.3 14.5 %collective-permute-done.9 = bf16[512,512]{0,1:T(8,128)(2,1)} collective-permute-done((bf16[512,512]{0,1:T(8,128)(2,1)S(1)}, bf16[512,512]{0,1:T(8,128)(2,1)}, u32[]{:S(2)}, u32[]{:S(2)}) %collective-permute-start.9) | collective-permute-done | bytes 524320 | tf_op jit(solution)/shard_map/ppermute | solution.py:31
  202.9 42.4 %all-gather.10.cloned.1.call-done = bf16[5376,1024]{1,0:T(8,128)(2,1)} async-done(((bf16[672,1024]{1,0:T(8,128)(2,1)}), bf16[5376,1024]{1,0:T(8,128)(2,1)}) %all-gather.10.cloned.1.call-update) | async-done | bytes 11010064 | tf_op jit(solution)/shard_map/all_gather | solution.py:76
  245.3 10.3 %convolution_bitcast_fusion = f32[64,8,8,128]{3,1,2,0:T(8,128)S(1)} fusion(bf16[512,5376]{0,1:T(8,128)(2,1)} %all-gather.6.cloned.1.call-done, bf16[5376,1024]{1,0:T(8,128)(2,1)} %all-gather.10.cloned.1.call-done), kind=kOutput, calls=%fused_computation.21 | convolution fusion | flops 5637144576 | bytes 18612224 | tf_op jit(solution)/shard_map/dot_general | solution.py:74
  259.0 11.8 %fusion.19 = f32[4,1536,512,2]{2,1,3,0:T(8,128)} fusion(bf16[512,4,128]{2,0,1:T(8,128)(2,1)S(1)} %maximum_convert_fusion, bf16[512,4,128]{2,0,1:T(8,128)(2,1)S(1)} %copy-done.5, bf16[512,4,128]{2,0,1:T(8,128)(2,1)S(1)} %copy-done.3, bf16[512,4,2,64]{3,0,2,1:T(8,128)(2,1)S(1)} %bitcast.54, bf16[512,4,2,64]{3,0,2,1:T(8,128)(2,1)S(1)} %bitcast.52), kind=kOutput, calls=%fused_computation.33 | convolution fusion | flops 1617428480 | bytes 27787264 | tf_op jit(solution)/shard_map/bhgd,khd->hgbk/dot_general | solution.py:57
  270.9 10.8 %fusion.32 = f32[4,2,512]{2,1,0:T(2,128)S(1)} fusion(pred[512,1536]{0,1:T(8,128)(4,1)} %fusion.11, bf16[512,4,128]{2,0,1:T(8,128)(2,1)S(1)} %maximum_convert_fusion, bf16[512,4,128]{2,0,1:T(8,128)(2,1)} %copy.33, bf16[512,4,128]{2,0,1:T(8,128)(2,1)S(1)} %copy-done.4, bf16[512,4,2,64]{3,0,2,1:T(8,128)(2,1)S(1)} %bitcast.55, ...), kind=kOutput, calls=%fused_computation.67 | convolution fusion | flops 1642595840 | bytes 3424256 | tf_op jit(solution)/shard_map/sub | solution.py:64
  281.6 15.4 %fusion.12 = bf16[4,128,2,512]{3,1,2,0:T(8,128)(2,1)} fusion(bf16[1536,4,128,1]{0,2,3,1:T(8,128)(2,1)} %bitcast.56, f32[4,2,512]{2,1,0:T(2,128)S(1)} %fusion.32, f32[4,1536,512,2]{2,1,3,0:T(8,128)} %fusion.19, pred[512,1536]{0,1:T(8,128)(4,1)} %fusion.11), kind=kOutput, calls=%fused_computation.24 | convolution fusion | flops 1642599936 | bytes 28590080 | tf_op jit(solution)/shard_map/hgbk,khd->bhgd/dot_general | solution.py:66
  297.1 17.6 %all-gather.14.cloned.1.call-done = bf16[4096,1344]{0,1:T(8,128)(2,1)} async-done(((bf16[512,1344]{0,1:T(8,128)(2,1)}), bf16[4096,1344]{0,1:T(8,128)(2,1)}) %all-gather.14.cloned.1.call-update) | async-done | bytes 11010064 | tf_op jit(solution)/shard_map/all_gather | solution.py:113
  314.6 82.2 %all-gather.12.cloned.1.call-done = bf16[512,4096]{0,1:T(8,128)(2,1)} async-done(((bf16[512,1024]{0,1:T(8,128)(2,1)}), bf16[512,4096]{0,1:T(8,128)(2,1)}) %all-gather.12.cloned.1.call-update) | async-done | bytes 4194320 | tf_op jit(solution)/shard_map/all_gather | solution.py:109
  396.9 10.7 %convolution_convert_fusion = bf16[512,1344]{0,1:T(8,128)(2,1)} fusion(bf16[4096,1344]{0,1:T(8,128)(2,1)} %all-gather.14.cloned.1.call-done, bf16[512,4096]{0,1:T(8,128)(2,1)} %all-gather.12.cloned.1.call-done), kind=kOutput, calls=%fused_computation.16 | convolution fusion | flops 5637832704 | bytes 16580608 | tf_op jit(solution)/shard_map/dot_general | solution.py:111
  (78 shorter events, 54.7 us)
Async XLA Ops:
  6.5 107.5 %all-gather.6.cloned.1.call-start = ((), (), s32[]{:S(2)}) async-start(), calls=%async_computation | async-start | bytes 6881280 | tf_op jit(solution)/shard_map/all_gather | solution.py:72
  7.3 157.9 %all-gather.8.cloned.1.call-start = ((), (), s32[]{:S(2)}) async-start(), calls=%async_computation.1 | async-start | bytes 6193152 | tf_op jit(solution)/shard_map/all_gather | solution.py:81
  8.0 237.3 %all-gather.10.cloned.1.call-start = ((), (), s32[]{:S(2)}) async-start(), calls=%async_computation.2 | async-start | bytes 12386304 | tf_op jit(solution)/shard_map/all_gather | solution.py:76
  8.7 305.9 %all-gather.14.cloned.1.call-start = ((), (), s32[]{:S(2)}) async-start(), calls=%async_computation.4 | async-start | bytes 12386304 | tf_op jit(solution)/shard_map/all_gather | solution.py:113
  9.3 387.5 %all-gather.12.cloned.1.call-start = ((), (), s32[]{:S(2)}) async-start(), calls=%async_computation.3 | async-start | bytes 5242880 | tf_op jit(solution)/shard_map/all_gather | solution.py:109
  9.4 12.2 %collective-permute-start = (bf16[672,512]{1,0:T(8,128)(2,1)}, bf16[672,512]{1,0:T(8,128)(2,1)S(1)}, u32[]{:S(2)}, u32[]{:S(2)}) collective-permute-start(bf16[672,512]{1,0:T(8,128)(2,1)} %param.10), channel_id=1, source_target_pairs={{0,28},{4,0},{8,4},{12,8},{16,12},{20,16},{24,20},{28,24},{1,29},{... | collective-permute-start | bytes 2064392 | tf_op jit(solution)/shard_map/ppermute | solution.py:16
  21.5 11.2 %collective-permute-start.1 = (bf16[672,512]{1,0:T(8,128)(2,1)S(1)}, bf16[672,512]{1,0:T(8,128)(2,1)S(1)}, u32[]{:S(2)}, u32[]{:S(2)}) collective-permute-start(bf16[672,512]{1,0:T(8,128)(2,1)S(1)} %collective-permute-done), channel_id=1, source_target_pairs={{0,28},{4,0},{8,4},{12,8},{16,12},{20,16},{24,20},{28,24},{1,29},{... | collective-permute-start | bytes 2064392 | tf_op jit(solution)/shard_map/ppermute | solution.py:16
  32.7 11.7 %collective-permute-start.2 = (bf16[672,512]{1,0:T(8,128)(2,1)S(1)}, bf16[672,512]{1,0:T(8,128)(2,1)S(1)}, u32[]{:S(2)}, u32[]{:S(2)}) collective-permute-start(bf16[672,512]{1,0:T(8,128)(2,1)S(1)} %collective-permute-done.1), channel_id=1, source_target_pairs={{0,28},{4,0},{8,4},{12,8},{16,12},{20,16},{24,20},{28,24},{1,29},{... | collective-permute-start | bytes 2064392 | tf_op jit(solution)/shard_map/ppermute | solution.py:16
  44.3 11.7 %collective-permute-start.3 = (bf16[672,512]{1,0:T(8,128)(2,1)S(1)}, bf16[672,512]{1,0:T(8,128)(2,1)S(1)}, u32[]{:S(2)}, u32[]{:S(2)}) collective-permute-start(bf16[672,512]{1,0:T(8,128)(2,1)S(1)} %collective-permute-done.2), channel_id=1, source_target_pairs={{0,28},{4,0},{8,4},{12,8},{16,12},{20,16},{24,20},{28,24},{1,29},{... | collective-permute-start | bytes 2064392 | tf_op jit(solution)/shard_map/ppermute | solution.py:16
  56.0 11.7 %collective-permute-start.4 = (bf16[672,512]{1,0:T(8,128)(2,1)S(1)}, bf16[672,512]{1,0:T(8,128)(2,1)S(1)}, u32[]{:S(2)}, u32[]{:S(2)}) collective-permute-start(bf16[672,512]{1,0:T(8,128)(2,1)S(1)} %collective-permute-done.3), channel_id=1, source_target_pairs={{0,28},{4,0},{8,4},{12,8},{16,12},{20,16},{24,20},{28,24},{1,29},{... | collective-permute-start | bytes 2064392 | tf_op jit(solution)/shard_map/ppermute | solution.py:16
  67.7 11.7 %collective-permute-start.5 = (bf16[672,512]{1,0:T(8,128)(2,1)S(1)}, bf16[672,512]{1,0:T(8,128)(2,1)S(1)}, u32[]{:S(2)}, u32[]{:S(2)}) collective-permute-start(bf16[672,512]{1,0:T(8,128)(2,1)S(1)} %collective-permute-done.4), channel_id=1, source_target_pairs={{0,28},{4,0},{8,4},{12,8},{16,12},{20,16},{24,20},{28,24},{1,29},{... | collective-permute-start | bytes 2064392 | tf_op jit(solution)/shard_map/ppermute | solution.py:16
  70.9 21.0 %copy-start = (bf16[672,512]{1,0:T(8,128)(2,1)S(1)}, bf16[672,512]{1,0:T(8,128)(2,1)}, u32[]{:S(2)}) copy-start(bf16[672,512]{1,0:T(8,128)(2,1)} %param.10) | copy-start | bytes 2064388
  79.3 11.7 %collective-permute-start.6 = (bf16[672,512]{1,0:T(8,128)(2,1)S(1)}, bf16[672,512]{1,0:T(8,128)(2,1)S(1)}, u32[]{:S(2)}, u32[]{:S(2)}) collective-permute-start(bf16[672,512]{1,0:T(8,128)(2,1)S(1)} %collective-permute-done.5), channel_id=1, source_target_pairs={{0,28},{4,0},{8,4},{12,8},{16,12},{20,16},{24,20},{28,24},{1,29},{... | collective-permute-start | bytes 2064392 | tf_op jit(solution)/shard_map/ppermute | solution.py:16
  122.2 50.1 %copy-start.6 = (f32[128]{0:T(128)S(1)}, f32[128]{0:T(128)}, u32[]{:S(2)}) copy-start(f32[128]{0:T(128)} %param.13) | copy-start | bytes 1540
  122.2 50.4 %copy-start.1 = (f32[512,64]{1,0:T(8,128)S(1)}, f32[512,64]{1,0:T(8,128)}, u32[]{:S(2)}) copy-start(f32[512,64]{1,0:T(8,128)} %get-tuple-element.9) | copy-start | bytes 393220
  122.2 50.4 %copy-start.2 = (f32[512,64]{1,0:T(8,128)S(1)}, f32[512,64]{1,0:T(8,128)}, u32[]{:S(2)}) copy-start(f32[512,64]{1,0:T(8,128)} %get-tuple-element.10) | copy-start | bytes 393220
  122.2 59.1 %collective-permute-start.7 = (bf16[512,512]{1,0:T(8,128)(2,1)}, bf16[512,512]{1,0:T(8,128)(2,1)}, u32[]{:S(2)}, u32[]{:S(2)}) collective-permute-start(bf16[512,512]{1,0:T(8,128)(2,1)} %fusion.16), channel_id=1, source_target_pairs={{0,8},{4,12},{8,16},{12,20},{16,24},{20,28},{1,9},{5,13},{9,17},{1... | collective-permute-start | bytes 1572872 | tf_op jit(solution)/shard_map/ppermute | solution.py:31
  126.5 54.8 %collective-permute-start.8 = (bf16[512,512]{1,0:T(8,128)(2,1)}, bf16[512,512]{1,0:T(8,128)(2,1)}, u32[]{:S(2)}, u32[]{:S(2)}) collective-permute-start(bf16[512,512]{1,0:T(8,128)(2,1)} %fusion.16), channel_id=1, source_target_pairs={{0,4},{4,8},{8,12},{12,16},{16,20},{20,24},{24,28},{1,5},{5,9},{9,... | collective-permute-start | bytes 1572872 | tf_op jit(solution)/shard_map/ppermute | solution.py:31
  173.5 25.3 %collective-permute-start.9 = (bf16[512,512]{0,1:T(8,128)(2,1)S(1)}, bf16[512,512]{0,1:T(8,128)(2,1)}, u32[]{:S(2)}, u32[]{:S(2)}) collective-permute-start(bf16[512,512]{0,1:T(8,128)(2,1)S(1)} %bitcast.59), channel_id=1, source_target_pairs={{0,8},{4,12},{8,16},{12,20},{16,24},{20,28},{1,9},{5,13},{9,17},{1... | collective-permute-start | bytes 1572872 | tf_op jit(solution)/shard_map/ppermute | solution.py:31
  176.6 24.2 %collective-permute-start.10 = (bf16[512,512]{0,1:T(8,128)(2,1)S(1)}, bf16[512,512]{0,1:T(8,128)(2,1)}, u32[]{:S(2)}, u32[]{:S(2)}) collective-permute-start(bf16[512,512]{0,1:T(8,128)(2,1)S(1)} %bitcast.60), channel_id=1, source_target_pairs={{0,4},{4,8},{8,12},{12,16},{16,20},{20,24},{24,28},{1,5},{5,9},{9,... | collective-permute-start | bytes 1572872 | tf_op jit(solution)/shard_map/ppermute | solution.py:31
  255.5 1.4 copy-start.7
  257.8 1.2 copy-start.3
  257.8 1.2 copy-start.5
  259.0 11.8 %copy-start.4 = (bf16[512,4,128]{2,0,1:T(8,128)(2,1)S(1)}, bf16[512,4,128]{2,0,1:T(8,128)(2,1)}, u32[]{:S(2)}) copy-start(bf16[512,4,128]{2,0,1:T(8,128)(2,1)} %copy.32) | copy-start | bytes 1572868
Sparse Core Ops, SparseCore 0:
  8.9 105.0 all-gather.5
  115.9 49.1 all-gather.7
  167.0 78.1 all-gather.9
  247.0 67.6 all-gather.13
  316.1 80.7 all-gather.11
